TPU v7x, 32 devices: a whole 2x2x4 slice. The times are simulated.
32 devices in a mesh: row: 4 (over x, core), col: 8 (over z, y).
Axes of the slice: x: 2, y: 2, z: 4, core: 2. Of those that a mesh axis runs over, the one named last changes fastest.
Arguments:
- features: bfloat16 [8192, 256], P(('col', 'row')), may hold values from -6 to 6
- weight: bfloat16 [256, 256], replicated, may hold values from -0.375 to 0.375
- grad_out: bfloat16 [8192, 256], P(('row', 'col')), may hold values from -6 to 6
- adj_values: bfloat16 [384, 1024, 128], P('row', 'col'), may hold values from -0.15625 to 0.15625
- block_pos: int32 [4, 768], P('row', 'col'), may hold values from 0 to 127, as said below
- block_count: int32 [4, 8], P('row', 'col'), may hold values from 24 to 96, as said below
Outputs:
- activation: bfloat16 [8192, 256], P(('row', 'col'))
- grad_input: bfloat16 [8192, 256], P(('col', 'row'))
- grad_weight: float32 [256, 256], replicated
Inputs may be any that keep to these rules, and one draw needn't show every extreme that they name: `block_pos`: within one tile the block positions of all 96 slots are distinct values below 128. `block_count`: some tile has exactly 96 live slots and some tile exactly 24.
All inputs are finite; a program needn't handle non-finite values.
Results may differ from a plain program's by a relative error of at most 0.018.
Values may be sent and summed in bfloat16 or wider, within the bound.
A program may use at most 128 MiB of HBM per device.

v0:
```python
import jax
import jax.numpy as jnp
from jax import lax
from jax.sharding import PartitionSpec as P


def tile_forward(values, positions, live_count, panel, row_blocks, col_blocks):
    slots = values.shape[0]
    block_size = values.shape[1]
    width = panel.shape[1]
    groups = 6
    per_group = slots // groups
    brow = positions // col_blocks
    bcol = positions % col_blocks
    live = (jnp.arange(slots, dtype=jnp.int32) < live_count).astype(jnp.float32)
    blocks = panel.reshape(col_blocks, block_size, width)

    def step(totals, items):
        vals, rows_idx, cols_idx, alive = items
        picked = blocks[cols_idx]
        prod = jnp.einsum("kij,kjf->kif", vals, picked, preferred_element_type=jnp.float32)
        onehot = (rows_idx[None, :] == jnp.arange(row_blocks, dtype=jnp.int32)[:, None]).astype(
            jnp.float32
        ) * alive[None, :]
        return (totals + jnp.einsum("bk,kif->bif", onehot, prod), None)

    items = (
        values.reshape(groups, per_group, block_size, block_size),
        brow.reshape(groups, per_group),
        bcol.reshape(groups, per_group),
        live.reshape(groups, per_group),
    )
    start = jnp.zeros((row_blocks, block_size, width), jnp.float32)
    totals, unused = lax.scan(step, start, items)
    return totals.reshape(row_blocks * block_size, width)


def tile_backward(values, positions, live_count, grads, row_blocks, col_blocks):
    slots = values.shape[0]
    block_size = values.shape[1]
    width = grads.shape[1]
    groups = 6
    per_group = slots // groups
    brow = positions // col_blocks
    bcol = positions % col_blocks
    live = (jnp.arange(slots, dtype=jnp.int32) < live_count).astype(jnp.float32)
    blocks = grads.reshape(row_blocks, block_size, width)

    def step(totals, items):
        vals, rows_idx, cols_idx, alive = items
        picked = blocks[rows_idx]
        prod = jnp.einsum("kij,kif->kjf", vals, picked, preferred_element_type=jnp.float32)
        onehot = (cols_idx[None, :] == jnp.arange(col_blocks, dtype=jnp.int32)[:, None]).astype(
            jnp.float32
        ) * alive[None, :]
        return (totals + jnp.einsum("bk,kjf->bjf", onehot, prod), None)

    items = (
        values.reshape(groups, per_group, block_size, block_size),
        brow.reshape(groups, per_group),
        bcol.reshape(groups, per_group),
        live.reshape(groups, per_group),
    )
    start = jnp.zeros((col_blocks, block_size, width), jnp.float32)
    totals, unused = lax.scan(step, start, items)
    return totals.reshape(col_blocks * block_size, width)


def body(features, weight, grad_out, adj_values, block_pos, block_count):
    block_size = adj_values.shape[2]
    rows_tile = grad_out.shape[0] * lax.axis_size("col")
    row_blocks = rows_tile // block_size
    projected = jnp.dot(features, weight, preferred_element_type=jnp.float32).astype(jnp.bfloat16)
    panel = lax.all_gather(projected, "row", axis=0, tiled=True)
    col_blocks = panel.shape[0] // block_size
    positions = block_pos[0]
    live_count = block_count[0, 0]
    partial_value = tile_forward(adj_values, positions, live_count, panel, row_blocks, col_blocks)
    hidden = lax.psum_scatter(
        partial_value.astype(jnp.bfloat16), "col", scatter_dimension=0, tiled=True
    ).astype(jnp.float32)
    sigma = jax.nn.sigmoid(hidden)
    activation = (hidden * sigma).astype(jnp.bfloat16)
    grad_hidden = (grad_out.astype(jnp.float32) * sigma * (1.0 + hidden * (1.0 - sigma))).astype(
        jnp.bfloat16
    )
    grad_panel = lax.all_gather(grad_hidden, "col", axis=0, tiled=True)
    partial_back = tile_backward(
        adj_values, positions, live_count, grad_panel, row_blocks, col_blocks
    )
    grad_xw = lax.psum_scatter(
        partial_back.astype(jnp.bfloat16), "row", scatter_dimension=0, tiled=True
    )
    local_weight = lax.dot_general(
        features, grad_xw, (((0,), (0,)), ((), ())), preferred_element_type=jnp.float32
    )
    grad_weight = lax.psum(local_weight, ("row", "col"))
    grad_input = lax.dot_general(
        grad_xw, weight, (((1,), (1,)), ((), ())), preferred_element_type=jnp.float32
    ).astype(jnp.bfloat16)
    return (activation, grad_input, grad_weight)


def solution(mesh):
    placed = (
        P(("col", "row"), None),
        P(),
        P(("row", "col"), None),
        P("row", "col", None),
        P("row", "col"),
        P("row", "col"),
    )
    return jax.shard_map(
        body,
        mesh=mesh,
        in_specs=placed,
        out_specs=(P(("row", "col"), None), P(("col", "row"), None), P()),
        check_vma=False,
    )
```

profile of v0, /device:TPU:0, one launch (start us, length us, event | category | flops | bytes accessed | tf_op | source)
XLA Modules:
  0.0 351.3 jit_solution(11104023459522061868)
XLA Ops:
  7.7 1.3 reduce.3
  9.8 1.1 convolution_convert_fusion.1
  10.9 8.6 %all_gather.6 = bf16[1024,256]{1,0:T(8,128)(2,1)S(1)} all-gather(bf16[256,256]{1,0:T(8,128)(2,1)S(1)} %convolution_convert_fusion.1), channel_id=1, replica_groups=mesh['row'=4,'col'=8] {'row'}, dimensions={0}, use_global_device_ids=true | all-gather | bytes 655360 | tf_op jit(solution)/shard_map/all_gather | solution.py:74
  19.6 33.6 %while.22 = (s32[]{:T(128)}, f32[16,128,256]{2,0,1:T(8,128)}, s32[6,16]{1,0:T(8,128)S(1)}, bf16[6,16]{1,0:T(8,128)(2,1)S(1)}, bf16[6,16,128,128]{3,2,1,0:T(8,128...) while((s32[]{:T(128)}, f32[16,128,256]{2,0,1:T(8,128)}, ...), condition=%wide.region_1.2_spmd.clone, body=%wide.region_0.1_spmd.clone.sunk | while | flops 152045104 | bytes 9966739 | solution.py:34
  19.6 0.6 gather_fusion
  20.2 1.5 fusion.77
  21.7 2.1 select_add_fusion.2
  24.5 1.5 fusion.77
  26.0 3.7 %select_add_fusion.2 = f32[16,128,256]{2,0,1:T(8,128)} fusion(f32[16,128,256]{2,0,1:T(8,128)} %get-tuple-element.261, bf16[16,128,256]{2,1,0:T(8,128)(2,1)S(1)} %fusion.77, pred[]{:T(512)S(6)} %compare.11, bf16[16]{0:T(256)(128)(2,1)S(1)} %fusion.78, s32[16]{0:T(128)S(1)} %fusion.79), kind=kOutput, calls=%fused_computation.4.clone.1 | convolution fusion | flops 17826304 | bytes 5242977 | tf_op jit(solution)/shard_map/while/body/eval_jaxpr/bk,kif->bif/dot_general | solution.py:25
  30.4 1.5 fusion.77
  31.9 3.7 %select_add_fusion.2 = f32[16,128,256]{2,0,1:T(8,128)} fusion(f32[16,128,256]{2,0,1:T(8,128)} %get-tuple-element.261, bf16[16,128,256]{2,1,0:T(8,128)(2,1)S(1)} %fusion.77, pred[]{:T(512)S(6)} %compare.11, bf16[16]{0:T(256)(128)(2,1)S(1)} %fusion.78, s32[16]{0:T(128)S(1)} %fusion.79), kind=kOutput, calls=%fused_computation.4.clone.1 | convolution fusion | flops 17826304 | bytes 5242977 | tf_op jit(solution)/shard_map/while/body/eval_jaxpr/bk,kif->bif/dot_general | solution.py:25
  35.6 0.6 gather_fusion
  36.2 1.5 fusion.77
  37.7 3.7 %select_add_fusion.2 = f32[16,128,256]{2,0,1:T(8,128)} fusion(f32[16,128,256]{2,0,1:T(8,128)} %get-tuple-element.261, bf16[16,128,256]{2,1,0:T(8,128)(2,1)S(1)} %fusion.77, pred[]{:T(512)S(6)} %compare.11, bf16[16]{0:T(256)(128)(2,1)S(1)} %fusion.78, s32[16]{0:T(128)S(1)} %fusion.79), kind=kOutput, calls=%fused_computation.4.clone.1 | convolution fusion | flops 17826304 | bytes 5242977 | tf_op jit(solution)/shard_map/while/body/eval_jaxpr/bk,kif->bif/dot_general | solution.py:25
  42.1 1.5 fusion.77
  43.6 3.7 %select_add_fusion.2 = f32[16,128,256]{2,0,1:T(8,128)} fusion(f32[16,128,256]{2,0,1:T(8,128)} %get-tuple-element.261, bf16[16,128,256]{2,1,0:T(8,128)(2,1)S(1)} %fusion.77, pred[]{:T(512)S(6)} %compare.11, bf16[16]{0:T(256)(128)(2,1)S(1)} %fusion.78, s32[16]{0:T(128)S(1)} %fusion.79), kind=kOutput, calls=%fused_computation.4.clone.1 | convolution fusion | flops 17826304 | bytes 5242977 | tf_op jit(solution)/shard_map/while/body/eval_jaxpr/bk,kif->bif/dot_general | solution.py:25
  48.0 1.5 fusion.77
  49.5 3.7 %select_add_fusion.2 = f32[16,128,256]{2,0,1:T(8,128)} fusion(f32[16,128,256]{2,0,1:T(8,128)} %get-tuple-element.261, bf16[16,128,256]{2,1,0:T(8,128)(2,1)S(1)} %fusion.77, pred[]{:T(512)S(6)} %compare.11, bf16[16]{0:T(256)(128)(2,1)S(1)} %fusion.78, s32[16]{0:T(128)S(1)} %fusion.79), kind=kOutput, calls=%fused_computation.4.clone.1 | convolution fusion | flops 17826304 | bytes 5242977 | tf_op jit(solution)/shard_map/while/body/eval_jaxpr/bk,kif->bif/dot_general | solution.py:25
  53.2 1.7 convert_element_type.39
  55.0 1.3 copy.11
  56.4 65.1 %reduce-scatter.3.cloned.1.call-done = bf16[256,256]{1,0:T(8,128)(2,1)} async-done(((bf16[2048,256]{1,0:T(8,128)(2,1)}), bf16[256,256]{1,0:T(8,128)(2,1)}) %reduce-scatter.3.cloned.1.call-update) | async-done | bytes 131088 | tf_op jit(solution)/shard_map/reduce_scatter | solution.py:79
  121.5 1.7 fusion.43
  123.3 40.2 %all-gather.2.cloned.1.call-done = bf16[2048,256]{1,0:T(8,128)(2,1)} async-done(((bf16[256,256]{1,0:T(8,128)(2,1)}), bf16[2048,256]{1,0:T(8,128)(2,1)}) %all-gather.2.cloned.1.call-update) | async-done | bytes 1048592 | tf_op jit(solution)/shard_map/all_gather | solution.py:87
  163.5 25.3 %while.23 = (s32[]{:T(128)}, f32[8,128,256]{2,0,1:T(8,128)S(1)}, s32[6,16]{1,0:T(8,128)S(1)}, bf16[6,16]{1,0:T(8,128)(2,1)S(1)}, bf16[6,16,128,128]{3,2,1,0:T(8,...) while((s32[]{:T(128)}, f32[8,128,256]{2,0,1:T(8,128)S(1)}, ...), condition=%wide.region_4.5_spmd.clone, body=%wide.region_3.4_spmd.clone.sunk | while | flops 143131952 | bytes 7869587 | solution.py:65
  163.5 1.8 gather_fusion.1
  165.4 1.5 fusion.85
  166.9 0.8 fusion.88
  167.7 1.8 gather_fusion.1
  169.6 1.5 fusion.85
  171.2 0.8 fusion.88
  172.0 1.8 gather_fusion.1
  173.8 1.5 fusion.85
  175.4 0.8 fusion.88
  176.2 1.8 gather_fusion.1
  178.0 1.5 fusion.85
  179.6 0.8 fusion.88
  180.4 1.8 gather_fusion.1
  182.3 1.5 fusion.85
  183.8 0.8 fusion.88
  184.7 1.8 gather_fusion.1
  186.5 1.5 fusion.85
  188.1 0.8 fusion.88
  188.9 1.1 copy.25
  190.0 20.4 %reduce-scatter.5.cloned.1.call-done = bf16[256,256]{1,0:T(8,128)(2,1)} async-done(((bf16[1024,256]{1,0:T(8,128)(2,1)}), bf16[256,256]{1,0:T(8,128)(2,1)}) %reduce-scatter.5.cloned.1.call-update) | async-done | bytes 131088 | tf_op jit(solution)/shard_map/reduce_scatter | solution.py:91
  210.5 1.8 convolution_bitcast_fusion
  212.3 1.8 convolution_convert_fusion
  214.1 128.9 %all-reduce.2.cloned.1.call-done = f32[256,256]{0,1:T(8,128)} async-done(((f32[256,256]{0,1:T(8,128)}), f32[256,256]{0,1:T(8,128)}) %all-reduce.2.cloned.1.call-update) | async-done | bytes 262160 | tf_op jit(solution)/shard_map/psum | solution.py:97
  343.0 1.8 copy.13
  (72 shorter events, 3.8 us)
Async XLA Ops:
  7.2 2.7 copy-start
  7.2 114.3 %reduce-scatter.3.cloned.1.call-start = ((), (), s32[]{:S(2)}) async-start(), calls=%async_computation.2 | async-start | bytes 1179648 | tf_op jit(solution)/shard_map/reduce_scatter | solution.py:79
  54.9 66.5 %copy-start.2 = (bf16[256,256]{1,0:T(8,128)(2,1)S(1)}, bf16[256,256]{1,0:T(8,128)(2,1)}, u32[]{:S(2)}) copy-start(bf16[256,256]{1,0:T(8,128)(2,1)} %param.12) | copy-start | bytes 393220
  56.3 107.2 %all-gather.2.cloned.1.call-start = ((), (), s32[]{:S(2)}) async-start(), calls=%async_computation.3 | async-start | bytes 1179648 | tf_op jit(solution)/shard_map/all_gather | solution.py:87
  123.2 87.3 %reduce-scatter.5.cloned.1.call-start = ((), (), s32[]{:S(2)}) async-start(), calls=%async_computation.4 | async-start | bytes 655360 | tf_op jit(solution)/shard_map/reduce_scatter | solution.py:91
  188.8 23.5 %copy-start.1 = (bf16[256,256]{1,0:T(8,128)(2,1)S(1)}, bf16[256,256]{1,0:T(8,128)(2,1)}, u32[]{:S(2)}) copy-start(bf16[256,256]{1,0:T(8,128)(2,1)} %param.11) | copy-start | bytes 393220
  190.0 153.0 %all-reduce.2.cloned.1.call-start = ((), (), s32[]{:S(2)}) async-start(), calls=%async_computation.5 | async-start | bytes 524288 | tf_op jit(solution)/shard_map/psum | solution.py:97
Sparse Core Ops, SparseCore 0:
  56.4 64.9 reduce-scatter.2
  124.2 39.3 all-gather.1
  190.1 20.3 reduce-scatter.4
  216.4 126.5 all-reduce.1
where the time goes:
time: 353 us; the launch traced here: 351 us
  waiting for transfers between devices  255 us (72%)
  matrix products  47.9 us (14%)
  local copies, waits for them, and re-layouts  19.8 us (6%)
  between operations  14.5 us (4%)
  blocking collectives  8.65 us (2%)
  other arithmetic  4.97 us (1%)
    psum x1, waiting for transfers between devices, body(): grad_weight = lax.psum(local_weight, ('row', 'col'))  129 us
    reduce_scatter x1, waiting for transfers between devices, body(): lax.psum_scatter(partial_value.astype(jnp.bfloat16), 'col', scatter_dimen...  65.1 us
    all_gather x1, waiting for transfers between devices, body(): grad_panel = lax.all_gather(grad_hidden, 'col', axis=0, tiled=True)  40.2 us
    dot_general x6, matrix products, step(): return (totals + jnp.einsum('bk,kif->bif', onehot, prod), None)  20.7 us
    reduce_scatter x1, waiting for transfers between devices, body(): lax.psum_scatter(partial_back.astype(jnp.bfloat16), 'row', scatter_dimens...  20.4 us
    gather x6, local copies, waits for them, and re-layouts, step(): picked = blocks[rows_idx]  11 us
    dot_general x6, matrix products, step(): jnp.einsum('kij,kif->kjf', vals, picked, preferred_element_type=jnp.float32)  9.18 us
    dot_general x6, matrix products, step(): jnp.einsum('kij,kjf->kif', vals, picked, preferred_element_type=jnp.float32)  8.8 us
  transfers between devices with their start and end apart: 4, of which 4 were waited for; matrix products, arithmetic and copies ran while one was open for 1% of the time, Pallas kernels for 0%

commit v1 on v0

--- a/solution.py
+++ b/solution.py
@@ -84,7 +84,12 @@
     grad_hidden = (grad_out.astype(jnp.float32) * sigma * (1.0 + hidden * (1.0 - sigma))).astype(
         jnp.bfloat16
     )
-    grad_panel = lax.all_gather(grad_hidden, "col", axis=0, tiled=True)
+    ring = [grad_hidden]
+    for hop in range(7):
+        ring.append(lax.ppermute(ring[-1], "col", [(dev, (dev + 1) % 8) for dev in range(8)]))
+    grad_panel = jnp.roll(
+        jnp.concatenate(ring[::-1], axis=0), (lax.axis_index("col") + 1) * ring[0].shape[0], axis=0
+    )
     partial_back = tile_backward(
         adj_values, positions, live_count, grad_panel, row_blocks, col_blocks
     )

time: 353 us -> 372 us (1.054)
  waiting for transfers between devices: 255 us -> 268 us
  matrix products: 47.9 us -> 59.4 us
  local copies, waits for them, and re-layouts: 19.8 us -> 14 us
    ppermute x0 -> x7, waiting for transfers between devices: none -> 54.5 us  [body(): lax.ppermute(ring[-1], 'col', [(dev, (dev + 1) % 8) for dev in range(8)])]
    all_gather x1 -> x0, waiting for transfers between devices: 40.2 us -> none  [body(): grad_panel = lax.all_gather(grad_hidden, 'col', axis=0, tiled=True)]
    dot_general x6, matrix products: 4.53 us -> 16.1 us  [step(): return (totals + jnp.einsum('bk,kjf->bjf', onehot, prod), None)]
    gather x6, local copies, waits for them, and re-layouts: 11 us -> 3.68 us  [step(): picked = blocks[rows_idx]]
  transfers between devices with their start and end apart: 4 -> 10, of which waited for: 4 -> 10; matrix products, arithmetic and copies ran while one was open for 1% -> 0% of each run, Pallas kernels for 0% -> 0%
where the time goes in v1:
time: 372 us; the launch traced here: 371 us
  waiting for transfers between devices  268 us (72%)
  matrix products  59.4 us (16%)
  between operations  14.6 us (4%)
  local copies, waits for them, and re-layouts  14 us (4%)
  blocking collectives  8.65 us (2%)
  other arithmetic  4.93 us (1%)
    psum x1, waiting for transfers between devices, body(): grad_weight = lax.psum(local_weight, ('row', 'col'))  129 us
    reduce_scatter x1, waiting for transfers between devices, body(): lax.psum_scatter(partial_value.astype(jnp.bfloat16), 'col', scatter_dimen...  65.2 us
    ppermute x7, waiting for transfers between devices, body(): lax.ppermute(ring[-1], 'col', [(dev, (dev + 1) % 8) for dev in range(8)])  54.5 us
    dot_general x6, matrix products, step(): return (totals + jnp.einsum('bk,kif->bif', onehot, prod), None)  20.6 us
    reduce_scatter x1, waiting for transfers between devices, body(): lax.psum_scatter(partial_back.astype(jnp.bfloat16), 'row', scatter_dimens...  19 us
    dot_general x6, matrix products, step(): return (totals + jnp.einsum('bk,kjf->bjf', onehot, prod), None)  16.1 us
    dot_general x6, matrix products, step(): jnp.einsum('kij,kif->kjf', vals, picked, preferred_element_type=jnp.float32)  9.2 us
    dot_general x6, matrix products, step(): jnp.einsum('kij,kjf->kif', vals, picked, preferred_element_type=jnp.float32)  8.78 us
  transfers between devices with their start and end apart: 10, of which 10 were waited for; matrix products, arithmetic and copies ran while one was open for 0% of the time, Pallas kernels for 0%

profile of v1, /device:TPU:0, one launch (start us, length us, event | category | flops | bytes accessed | tf_op | source)
XLA Modules:
  0.0 370.9 jit_solution(15227586706198496337)
XLA Ops:
  7.7 1.3 reduce.3
  9.8 1.1 convolution_convert_fusion.1
  10.9 8.6 %all_gather.3 = bf16[1024,256]{1,0:T(8,128)(2,1)S(1)} all-gather(bf16[256,256]{1,0:T(8,128)(2,1)S(1)} %convolution_convert_fusion.1), channel_id=1, replica_groups=mesh['row'=4,'col'=8] {'row'}, dimensions={0}, use_global_device_ids=true | all-gather | bytes 655360 | tf_op jit(solution)/shard_map/all_gather | solution.py:74
  19.6 33.5 %while.22 = (s32[]{:T(128)}, f32[16,128,256]{2,0,1:T(8,128)}, s32[6,16]{1,0:T(8,128)S(1)}, bf16[6,16]{1,0:T(8,128)(2,1)S(1)}, bf16[6,16,128,128]{3,2,1,0:T(8,128...) while((s32[]{:T(128)}, f32[16,128,256]{2,0,1:T(8,128)}, ...), condition=%wide.region_1.2_spmd.clone, body=%wide.region_0.1_spmd.clone.sunk | while | flops 152045104 | bytes 9966739 | solution.py:34
  20.2 1.5 fusion.77
  21.7 2.1 select_add_fusion.2
  24.5 1.5 fusion.77
  26.0 3.7 select_add_fusion.2
  30.3 1.5 fusion.77
  31.8 3.7 select_add_fusion.2
  36.2 1.5 fusion.77
  37.7 3.7 select_add_fusion.2
  42.0 1.5 fusion.77
  43.5 3.7 select_add_fusion.2
  47.9 1.5 fusion.77
  49.4 3.7 select_add_fusion.2
  53.1 1.7 convert_element_type.39
  54.8 1.3 copy.11
  56.2 65.2 %reduce-scatter.3.cloned.1.call-done = bf16[256,256]{1,0:T(8,128)(2,1)} async-done(((bf16[2048,256]{1,0:T(8,128)(2,1)}), bf16[256,256]{1,0:T(8,128)(2,1)}) %reduce-scatter.3.cloned.1.call-update) | async-done | bytes 131088 | tf_op jit(solution)/shard_map/reduce_scatter | solution.py:79
  121.4 1.7 fusion.43
  123.1 1.1 collective-permute-start
  124.1 6.6 %collective-permute-done = bf16[256,256]{1,0:T(8,128)(2,1)S(1)} collective-permute-done((bf16[256,256]{1,0:T(8,128)(2,1)S(1)}, bf16[256,256]{1,0:T(8,128)(2,1)S(1)}, u32[]{:S(2)}, u32[]{:S(2)}) %collective-permute-start) | collective-permute-done | bytes 131104 | tf_op jit(solution)/shard_map/ppermute | solution.py:89
  130.7 7.7 %collective-permute-done.1 = bf16[256,256]{1,0:T(8,128)(2,1)S(1)} collective-permute-done((bf16[256,256]{1,0:T(8,128)(2,1)S(1)}, bf16[256,256]{1,0:T(8,128)(2,1)S(1)}, u32[]{:S(2)}, u32[]{:S(2)}) %collective-permute-start.1) | collective-permute-done | bytes 131104 | tf_op jit(solution)/shard_map/ppermute | solution.py:89
  138.4 7.8 %collective-permute-done.2 = bf16[256,256]{1,0:T(8,128)(2,1)S(1)} collective-permute-done((bf16[256,256]{1,0:T(8,128)(2,1)S(1)}, bf16[256,256]{1,0:T(8,128)(2,1)S(1)}, u32[]{:S(2)}, u32[]{:S(2)}) %collective-permute-start.2) | collective-permute-done | bytes 131104 | tf_op jit(solution)/shard_map/ppermute | solution.py:89
  146.2 8.9 %collective-permute-done.3 = bf16[256,256]{1,0:T(8,128)(2,1)S(1)} collective-permute-done((bf16[256,256]{1,0:T(8,128)(2,1)S(1)}, bf16[256,256]{1,0:T(8,128)(2,1)S(1)}, u32[]{:S(2)}, u32[]{:S(2)}) %collective-permute-start.3) | collective-permute-done | bytes 131104 | tf_op jit(solution)/shard_map/ppermute | solution.py:89
  155.1 8.2 %collective-permute-done.4 = bf16[256,256]{1,0:T(8,128)(2,1)S(1)} collective-permute-done((bf16[256,256]{1,0:T(8,128)(2,1)S(1)}, bf16[256,256]{1,0:T(8,128)(2,1)S(1)}, u32[]{:S(2)}, u32[]{:S(2)}) %collective-permute-start.4) | collective-permute-done | bytes 131104 | tf_op jit(solution)/shard_map/ppermute | solution.py:89
  163.3 7.7 %collective-permute-done.5 = bf16[256,256]{1,0:T(8,128)(2,1)S(1)} collective-permute-done((bf16[256,256]{1,0:T(8,128)(2,1)S(1)}, bf16[256,256]{1,0:T(8,128)(2,1)S(1)}, u32[]{:S(2)}, u32[]{:S(2)}) %collective-permute-start.5) | collective-permute-done | bytes 131104 | tf_op jit(solution)/shard_map/ppermute | solution.py:89
  171.0 7.7 %collective-permute-done.6 = bf16[256,256]{1,0:T(8,128)(2,1)S(1)} collective-permute-done((bf16[256,256]{1,0:T(8,128)(2,1)S(1)}, bf16[256,256]{1,0:T(8,128)(2,1)S(1)}, u32[]{:S(2)}, u32[]{:S(2)}) %collective-permute-start.6) | collective-permute-done | bytes 131104 | tf_op jit(solution)/shard_map/ppermute | solution.py:89
  179.0 29.4 %while.23 = (s32[]{:T(128)}, f32[8,128,256]{2,0,1:T(8,128)}, s32[6,16]{1,0:T(8,128)S(1)}, bf16[6,16]{1,0:T(8,128)(2,1)S(1)}, bf16[6,16,128,128]{3,2,1,0:T(8,128)...) while((s32[]{:T(128)}, f32[8,128,256]{2,0,1:T(8,128)}, ...), condition=%wide.region_4.5_spmd.clone, body=%wide.region_3.4_spmd.clone.sunk | while | flops 143131952 | bytes 7869587 | solution.py:65
  179.1 0.6 gather_fusion.1
  179.7 1.5 fusion.85
  181.3 1.7 fusion.88
  183.6 1.5 fusion.85
  185.1 2.9 fusion.88
  188.7 1.5 fusion.85
  190.2 2.9 fusion.88
  193.8 1.5 fusion.85
  195.3 2.9 fusion.88
  198.9 1.5 fusion.85
  200.4 2.9 fusion.88
  203.9 1.5 fusion.85
  205.5 2.9 fusion.88
  208.4 2.4 copy.25
  210.9 19.0 %reduce-scatter.5.cloned.1.call-done = bf16[256,256]{1,0:T(8,128)(2,1)} async-done(((bf16[1024,256]{1,0:T(8,128)(2,1)}), bf16[256,256]{1,0:T(8,128)(2,1)}) %reduce-scatter.5.cloned.1.call-update) | async-done | bytes 131088 | tf_op jit(solution)/shard_map/reduce_scatter | solution.py:96
  229.9 1.8 convolution_bitcast_fusion
  231.7 1.8 convolution_convert_fusion
  233.5 129.1 %all-reduce.2.cloned.1.call-done = f32[256,256]{0,1:T(8,128)} async-done(((f32[256,256]{0,1:T(8,128)}), f32[256,256]{0,1:T(8,128)}) %all-reduce.2.cloned.1.call-update) | async-done | bytes 262160 | tf_op jit(solution)/shard_map/psum | solution.py:102
  362.6 1.8 copy.13
  (100 shorter events, 8.2 us)
Async XLA Ops:
  7.2 2.7 copy-start
  7.2 114.2 %reduce-scatter.3.cloned.1.call-start = ((), (), s32[]{:S(2)}) async-start(), calls=%async_computation.2 | async-start | bytes 1179648 | tf_op jit(solution)/shard_map/reduce_scatter | solution.py:79
  54.8 66.6 %copy-start.2 = (bf16[256,256]{1,0:T(8,128)(2,1)S(1)}, bf16[256,256]{1,0:T(8,128)(2,1)}, u32[]{:S(2)}) copy-start(bf16[256,256]{1,0:T(8,128)(2,1)} %param.12) | copy-start | bytes 393220
  56.2 173.7 %reduce-scatter.5.cloned.1.call-start = ((), (), s32[]{:S(2)}) async-start(), calls=%async_computation.3 | async-start | bytes 655360 | tf_op jit(solution)/shard_map/reduce_scatter | solution.py:96
  123.1 7.7 %collective-permute-start = (bf16[256,256]{1,0:T(8,128)(2,1)S(1)}, bf16[256,256]{1,0:T(8,128)(2,1)S(1)}, u32[]{:S(2)}, u32[]{:S(2)}) collective-permute-start(bf16[256,256]{1,0:T(8,128)(2,1)S(1)} %get-tuple-element.161), channel_id=1, source_target_pairs={{0,1},{1,2},{2,3},{3,4},{4,5},{5,6},{6,7},{7,0},{8,9},{9,10},{10,1... | collective-permute-start | bytes 393224 | tf_op jit(solution)/shard_map/ppermute | solution.py:89
  130.7 7.7 %collective-permute-start.1 = (bf16[256,256]{1,0:T(8,128)(2,1)S(1)}, bf16[256,256]{1,0:T(8,128)(2,1)S(1)}, u32[]{:S(2)}, u32[]{:S(2)}) collective-permute-start(bf16[256,256]{1,0:T(8,128)(2,1)S(1)} %collective-permute-done), channel_id=1, source_target_pairs={{0,1},{1,2},{2,3},{3,4},{4,5},{5,6},{6,7},{7,0},{8,9},{9,10},{10,1... | collective-permute-start | bytes 393224 | tf_op jit(solution)/shard_map/ppermute | solution.py:89
  138.4 7.8 %collective-permute-start.2 = (bf16[256,256]{1,0:T(8,128)(2,1)S(1)}, bf16[256,256]{1,0:T(8,128)(2,1)S(1)}, u32[]{:S(2)}, u32[]{:S(2)}) collective-permute-start(bf16[256,256]{1,0:T(8,128)(2,1)S(1)} %collective-permute-done.1), channel_id=1, source_target_pairs={{0,1},{1,2},{2,3},{3,4},{4,5},{5,6},{6,7},{7,0},{8,9},{9,10},{10,1... | collective-permute-start | bytes 393224 | tf_op jit(solution)/shard_map/ppermute | solution.py:89
  146.2 8.9 %collective-permute-start.3 = (bf16[256,256]{1,0:T(8,128)(2,1)S(1)}, bf16[256,256]{1,0:T(8,128)(2,1)S(1)}, u32[]{:S(2)}, u32[]{:S(2)}) collective-permute-start(bf16[256,256]{1,0:T(8,128)(2,1)S(1)} %collective-permute-done.2), channel_id=1, source_target_pairs={{0,1},{1,2},{2,3},{3,4},{4,5},{5,6},{6,7},{7,0},{8,9},{9,10},{10,1... | collective-permute-start | bytes 393224 | tf_op jit(solution)/shard_map/ppermute | solution.py:89
  155.1 8.2 %collective-permute-start.4 = (bf16[256,256]{1,0:T(8,128)(2,1)S(1)}, bf16[256,256]{1,0:T(8,128)(2,1)S(1)}, u32[]{:S(2)}, u32[]{:S(2)}) collective-permute-start(bf16[256,256]{1,0:T(8,128)(2,1)S(1)} %collective-permute-done.3), channel_id=1, source_target_pairs={{0,1},{1,2},{2,3},{3,4},{4,5},{5,6},{6,7},{7,0},{8,9},{9,10},{10,1... | collective-permute-start | bytes 393224 | tf_op jit(solution)/shard_map/ppermute | solution.py:89
  163.3 7.7 %collective-permute-start.5 = (bf16[256,256]{1,0:T(8,128)(2,1)S(1)}, bf16[256,256]{1,0:T(8,128)(2,1)S(1)}, u32[]{:S(2)}, u32[]{:S(2)}) collective-permute-start(bf16[256,256]{1,0:T(8,128)(2,1)S(1)} %collective-permute-done.4), channel_id=1, source_target_pairs={{0,1},{1,2},{2,3},{3,4},{4,5},{5,6},{6,7},{7,0},{8,9},{9,10},{10,1... | collective-permute-start | bytes 393224 | tf_op jit(solution)/shard_map/ppermute | solution.py:89
  171.0 7.7 %collective-permute-start.6 = (bf16[256,256]{1,0:T(8,128)(2,1)S(1)}, bf16[256,256]{1,0:T(8,128)(2,1)S(1)}, u32[]{:S(2)}, u32[]{:S(2)}) collective-permute-start(bf16[256,256]{1,0:T(8,128)(2,1)S(1)} %collective-permute-done.5), channel_id=1, source_target_pairs={{0,1},{1,2},{2,3},{3,4},{4,5},{5,6},{6,7},{7,0},{8,9},{9,10},{10,1... | collective-permute-start | bytes 393224 | tf_op jit(solution)/shard_map/ppermute | solution.py:89
  208.4 23.3 %copy-start.1 = (bf16[256,256]{1,0:T(8,128)(2,1)S(1)}, bf16[256,256]{1,0:T(8,128)(2,1)}, u32[]{:S(2)}) copy-start(bf16[256,256]{1,0:T(8,128)(2,1)} %param.11) | copy-start | bytes 393220
  210.8 151.8 %all-reduce.2.cloned.1.call-start = ((), (), s32[]{:S(2)}) async-start(), calls=%async_computation.4 | async-start | bytes 524288 | tf_op jit(solution)/shard_map/psum | solution.py:102
Sparse Core Ops, SparseCore 0:
  56.3 65.0 reduce-scatter.2
  210.9 18.8 reduce-scatter.4
  235.9 126.5 all-reduce.1
